TPU v7x, 32 devices: a whole 2x2x4 slice. The times are simulated.
32 devices in a mesh: ctx: 4 (over y, core), tp: 4 (over z), dp: 2 (over x).
Axes of the slice: x: 2, y: 2, z: 4, core: 2. Of those that a mesh axis runs over, the one named last changes fastest.
Arguments:
- tokens: bfloat16 [3072, 3584], P(('dp', 'ctx'), 'tp'), may hold values from -6 to 6
- expert_ids: int32 [3072, 8], P(('dp', 'ctx')), may hold values from 0 to 255, all different within a row; in each aligned block of 384 rows (0 to 383, 384 to 767, ...) at most 24 rows name the same one
- gate_codes: int32 [3072, 8], P(('dp', 'ctx')), may hold values from 1 to 32767
- up_weight: bfloat16 [4, 3584, 1024], P('ctx', 'tp', 'dp'), may hold values from -0.09375 to 0.09375
- down_weight: bfloat16 [4, 1024, 3584], P('ctx', 'dp', 'tp'), may hold values from -0.1875 to 0.1875
- cotangent: bfloat16 [3072, 3584], P(('dp', 'ctx'), 'tp'), may hold values from -6 to 6
Outputs:
- mixed: bfloat16 [3072, 3584], P(('dp', 'ctx'), 'tp')
- grad_tokens: bfloat16 [3072, 3584], P(('dp', 'ctx'), 'tp')
- grad_up: bfloat16 [4, 3584, 1024], P('ctx', 'tp', 'dp')
- grad_down: bfloat16 [4, 1024, 3584], P('ctx', 'dp', 'tp')
Inputs may be any that keep to these rules, and one draw needn't show every extreme that they name: `expert_ids`: each row names 8 different experts; among the 384 rows of one device no expert is named more than 24 times.
All inputs are finite; a program needn't handle non-finite values.
Results may differ from a plain program's by a relative error of at most 0.0066.
Values may be sent and summed in bfloat16 or wider, within the bound.
A program may use at most 64 MiB of HBM per device.

v0:
```python
import jax
import jax.numpy as jnp
from jax import lax
from jax.sharding import PartitionSpec as P


def place_slots(expert_ids, gate_codes, experts, capacity):
    rows_count, picks = expert_ids.shape
    flat_ids = expert_ids.reshape(-1)
    one_hot = (flat_ids[:, None] == jnp.arange(experts, dtype=jnp.int32)[None, :]).astype(jnp.int32)
    before = jnp.cumsum(one_hot, axis=0) - one_hot
    slot_rank = jnp.sum(before * one_hot, axis=1)
    inside = flat_ids < experts
    target = jnp.where(inside, flat_ids * capacity + slot_rank, experts * capacity)
    source = jnp.arange(rows_count * picks, dtype=jnp.int32) // picks
    slot_token = (
        jnp.full((experts * capacity,), rows_count, jnp.int32).at[target].set(source, mode="drop")
    )
    weights = gate_codes.reshape(-1).astype(jnp.float32) / 32768.0
    gate_slot = jnp.zeros((experts * capacity,), jnp.float32).at[target].set(weights, mode="drop")
    return (slot_token, gate_slot)


def silu_grad(values):
    sigma = jax.nn.sigmoid(values)
    return sigma * (1.0 + values * (1.0 - sigma))


def body(tokens, expert_ids, gate_codes, up_weight, down_weight, cotangent):
    sources = lax.axis_size("ctx")
    rows_count, features = tokens.shape
    capacity = rows_count // 16
    slot_token, gate_slot = place_slots(expert_ids, gate_codes, sources, capacity)
    padded_x = jnp.concatenate([tokens, jnp.zeros((1, features), tokens.dtype)], axis=0)
    outgoing = padded_x[slot_token].reshape(sources, capacity, features)
    arrived = lax.all_to_all(outgoing, "ctx", split_axis=0, concat_axis=0, tiled=True).reshape(
        sources * capacity, features
    )
    w_up, w_down = (
        lax.all_gather(up_weight[0], "dp", axis=1, tiled=True),
        lax.all_gather(down_weight[0], "dp", axis=0, tiled=True),
    )
    hidden = lax.psum(jnp.dot(arrived, w_up, preferred_element_type=jnp.float32), "tp")
    active = jax.nn.silu(hidden).astype(jnp.bfloat16)
    produced = jnp.dot(active, w_down, preferred_element_type=jnp.float32).astype(jnp.bfloat16)
    returned = lax.all_to_all(
        produced.reshape(sources, capacity, features),
        "ctx",
        split_axis=0,
        concat_axis=0,
        tiled=True,
    ).reshape(sources * capacity, features)
    mixed = (
        jnp.zeros((rows_count + 1, features), jnp.float32)
        .at[slot_token]
        .add(gate_slot[:, None] * returned.astype(jnp.float32))
    )
    mixed = mixed[:rows_count].astype(jnp.bfloat16)
    padded_c = jnp.concatenate([cotangent, jnp.zeros((1, features), cotangent.dtype)], axis=0)
    grad_send = (gate_slot[:, None] * padded_c[slot_token].astype(jnp.float32)).astype(jnp.bfloat16)
    grad_rows = lax.all_to_all(
        grad_send.reshape(sources, capacity, features),
        "ctx",
        split_axis=0,
        concat_axis=0,
        tiled=True,
    ).reshape(sources * capacity, features)
    contract_last = (((1,), (1,)), ((), ()))
    contract_first = (((0,), (0,)), ((), ()))
    grad_act = lax.psum(
        lax.dot_general(grad_rows, w_down, contract_last, preferred_element_type=jnp.float32), "tp"
    )
    grad_hid = (grad_act * silu_grad(hidden)).astype(jnp.bfloat16)
    grad_in = lax.dot_general(
        grad_hid, w_up, contract_last, preferred_element_type=jnp.float32
    ).astype(jnp.bfloat16)
    back_rows = lax.all_to_all(
        grad_in.reshape(sources, capacity, features), "ctx", split_axis=0, concat_axis=0, tiled=True
    ).reshape(sources * capacity, features)
    grad_tokens = (
        jnp.zeros((rows_count + 1, features), jnp.float32)
        .at[slot_token]
        .add(back_rows.astype(jnp.float32))
    )
    grad_tokens = grad_tokens[:rows_count].astype(jnp.bfloat16)
    part_up = lax.dot_general(arrived, grad_hid, contract_first, preferred_element_type=jnp.float32)
    part_down = lax.dot_general(
        active, grad_rows, contract_first, preferred_element_type=jnp.float32
    )
    grad_up, grad_down = (
        lax.psum_scatter(
            part_up.astype(jnp.bfloat16), "dp", scatter_dimension=1, tiled=True
        ).astype(jnp.float32),
        lax.psum_scatter(
            part_down.astype(jnp.bfloat16), "dp", scatter_dimension=0, tiled=True
        ).astype(jnp.float32),
    )
    return (
        mixed,
        grad_tokens,
        grad_up.astype(jnp.bfloat16)[None],
        grad_down.astype(jnp.bfloat16)[None],
    )


def solution(mesh):
    return jax.shard_map(
        body,
        mesh=mesh,
        in_specs=(
            P(("dp", "ctx"), "tp"),
            P(("dp", "ctx"), None),
            P(("dp", "ctx"), None),
            P("ctx", "tp", "dp"),
            P("ctx", "dp", "tp"),
            P(("dp", "ctx"), "tp"),
        ),
        out_specs=(
            P(("dp", "ctx"), "tp"),
            P(("dp", "ctx"), "tp"),
            P("ctx", "tp", "dp"),
            P("ctx", "dp", "tp"),
        ),
        check_vma=False,
    )
```

profile of v0, /device:TPU:0, one launch (start us, length us, event | category | flops | bytes accessed | tf_op | source)
XLA Modules:
  0.0 190.8 jit_solution(14327130908680088390)
XLA Ops:
  9.7 1.2 reduce-window.6
  11.6 11.8 %scatter_custom_fusion = s32[96]{0:T(128)S(1)} fusion(s32[3072]{0:T(1024)S(1)} %bitcast.64, s32[3072]{0:T(1024)S(1)} %add_select_fusion, s32[]{:T(128)} %constant.17.clone.1), kind=kCustom, calls=%fused_computation.56 | custom fusion | bytes 388 | tf_op jit(solution)/shard_map/scatter | solution.py:17
  23.4 1.5 gather_fusion
  24.9 4.3 %all-to-all-start = ((bf16[4,24,896]{2,1,0:T(8,128)(2,1)}), bf16[4,24,896]{2,1,0:T(8,128)(2,1)S(1)}, u32[]{:S(2)}, u32[]{:S(2)}) async-start(bf16[4,24,896]{2,1,0:T(8,128)(2,1)} %bitcast.3), calls=%async_computation | async-start | bytes 344064 | tf_op jit(solution)/shard_map/all_to_all | solution.py:36
  29.4 11.8 %scatter_custom_fusion.1 = f32[96]{0:T(128)S(1)} fusion(s32[3072]{0:T(1024)S(1)} %bitcast.65, f32[3072]{0:T(1024)S(1)} %reshape.139, f32[]{:T(128)} %constant.15.clone.1), kind=kCustom, calls=%fused_computation.54 | custom fusion | bytes 388 | tf_op jit(solution)/shard_map/scatter | solution.py:20
  42.9 3.4 %all-to-all-start.2 = ((bf16[4,24,896]{2,1,0:T(8,128)(2,1)}), bf16[4,24,896]{2,1,0:T(8,128)(2,1)S(1)}, u32[]{:S(2)}, u32[]{:S(2)}) async-start(bf16[4,24,896]{2,1,0:T(8,128)(2,1)} %fusion.19), calls=%async_computation.2 | async-start | bytes 344064 | tf_op jit(solution)/shard_map/all_to_all | solution.py:61
  46.3 2.7 %fusion.6 = f32[96,1024]{1,0:T(8,128)} fusion(bf16[96,896]{1,0:T(8,128)(2,1)S(1)} %bitcast.56, bf16[1,896,1024]{2,1,0:T(8,128)(2,1)} %all-gather.5.cloned.1.call-done), kind=kOutput, calls=%fused_computation.12 | convolution fusion | flops 176160768 | bytes 2400256 | tf_op jit(solution)/shard_map/dot_general | solution.py:43
  49.0 2.3 %all-to-all-done.2 = bf16[4,24,896]{2,1,0:T(8,128)(2,1)S(1)} async-done(((bf16[4,24,896]{2,1,0:T(8,128)(2,1)}), bf16[4,24,896]{2,1,0:T(8,128)(2,1)S(1)}, u32[]{:S(2)}, u32[]{:S(2)}) %all-to-all-start.2) | async-done | bytes 172064 | tf_op jit(solution)/shard_map/all_to_all | solution.py:61
  51.3 22.8 %all-gather.7.cloned.1.call-done = bf16[1,1024,896]{2,1,0:T(8,128)(2,1)} async-done(((bf16[1,512,896]{2,1,0:T(8,128)(2,1)}), bf16[1,1024,896]{2,1,0:T(8,128)(2,1)}) %all-gather.7.cloned.1.call-update) | async-done | bytes 1835024 | tf_op jit(solution)/shard_map/all_gather | solution.py:41
  74.1 2.9 %fusion = f32[96,1024]{1,0:T(8,128)} fusion(bf16[96,896]{1,0:T(8,128)(2,1)S(1)} %bitcast.58, bf16[1,1024,896]{2,1,0:T(8,128)(2,1)} %all-gather.7.cloned.1.call-done), kind=kOutput, calls=%fused_computation.6 | convolution fusion | flops 176160768 | bytes 2400256 | tf_op jit(solution)/shard_map/dot_general | solution.py:71
  77.2 44.0 %all-reduce.5.cloned.1.call-done = (f32[96,1024]{1,0:T(8,128)}, f32[96,1024]{1,0:T(8,128)}) async-done(((f32[96,1024]{1,0:T(8,128)}, f32[96,1024]{1,0:T(8,128)}), (f32[96,1024]{1,0:T(8,128)}, f32[96,1024]{1,0:T(8,128)})) %all-reduce.5.cloned.1.call-update) | async-done | bytes 786448 | tf_op jit(solution)/shard_map/psum | solution.py:43
  121.2 3.0 %convolution_convert_fusion = bf16[1024,896]{1,0:T(8,128)(2,1)} fusion(bf16[96,896]{1,0:T(8,128)(2,1)S(1)} %bitcast.59, f32[96,1024]{1,0:T(8,128)} %get-tuple-element.4), kind=kOutput, calls=%fused_computation.14 | convolution fusion | flops 177569792 | bytes 2400256 | tf_op jit(solution)/shard_map/dot_general | solution.py:87
  124.4 1.9 %convolution_convert_fusion.1 = bf16[896,1024]{1,0:T(8,128)(2,1)} fusion(bf16[96,896]{1,0:T(8,128)(2,1)S(1)} %bitcast.57, bf16[96,1024]{1,0:T(8,128)(2,1)S(1)} %multiply_convert_fusion), kind=kOutput, calls=%fused_computation.15 | convolution fusion | flops 177078272 | bytes 2203648 | tf_op jit(solution)/shard_map/dot_general | solution.py:86
  126.4 2.8 %fusion.11 = bf16[96,896]{1,0:T(8,128)(2,1)} fusion(bf16[1,1024,896]{2,1,0:T(8,128)(2,1)} %all-gather.7.cloned.1.call-done, f32[96,1024]{1,0:T(8,128)S(1)} %copy-done.1), kind=kOutput, calls=%fused_computation.19 | convolution fusion | flops 176738304 | bytes 2400256 | tf_op jit(solution)/shard_map/dot_general | solution.py:45
  129.1 3.4 %all-to-all-start.1 = ((bf16[4,24,896]{2,1,0:T(8,128)(2,1)}), bf16[4,24,896]{2,1,0:T(8,128)(2,1)S(1)}, u32[]{:S(2)}, u32[]{:S(2)}) async-start(bf16[4,24,896]{2,1,0:T(8,128)(2,1)} %bitcast.7), calls=%async_computation.1 | async-start | bytes 344064 | tf_op jit(solution)/shard_map/all_to_all | solution.py:46
  132.5 1.3 fusion.8
  133.8 3.7 %all-to-all-done.1 = bf16[4,24,896]{2,1,0:T(8,128)(2,1)S(1)} async-done(((bf16[4,24,896]{2,1,0:T(8,128)(2,1)}), bf16[4,24,896]{2,1,0:T(8,128)(2,1)S(1)}, u32[]{:S(2)}, u32[]{:S(2)}) %all-to-all-start.1) | async-done | bytes 172064 | tf_op jit(solution)/shard_map/all_to_all | solution.py:46
  137.5 3.3 %all-to-all-start.3 = ((bf16[4,24,896]{2,1,0:T(8,128)(2,1)}), bf16[4,24,896]{2,1,0:T(8,128)(2,1)S(1)}, u32[]{:S(2)}, u32[]{:S(2)}) async-start(bf16[4,24,896]{2,1,0:T(8,128)(2,1)} %bitcast.11), calls=%async_computation.3 | async-start | bytes 344064 | tf_op jit(solution)/shard_map/all_to_all | solution.py:77
  140.8 1.8 scatter_custom_fusion.2
  142.6 0.9 slice.29
  143.6 2.3 %all-to-all-done.3 = bf16[4,24,896]{2,1,0:T(8,128)(2,1)S(1)} async-done(((bf16[4,24,896]{2,1,0:T(8,128)(2,1)}), bf16[4,24,896]{2,1,0:T(8,128)(2,1)S(1)}, u32[]{:S(2)}, u32[]{:S(2)}) %all-to-all-start.3) | async-done | bytes 172064 | tf_op jit(solution)/shard_map/all_to_all | solution.py:77
  145.9 1.7 scatter_custom_fusion.3
  148.5 4.1 %reduce-scatter.5.cloned.1.call-done = bf16[512,896]{1,0:T(8,128)(2,1)} async-done(((bf16[1024,896]{1,0:T(8,128)(2,1)}), bf16[512,896]{1,0:T(8,128)(2,1)}) %reduce-scatter.5.cloned.1.call-update) | async-done | bytes 917520 | tf_op jit(solution)/shard_map/reduce_scatter | solution.py:94
  152.5 31.7 %reduce-scatter.3.cloned.1.call-done = bf16[896,512]{1,0:T(8,128)(2,1)} async-done(((bf16[896,1024]{1,0:T(8,128)(2,1)}), bf16[896,512]{1,0:T(8,128)(2,1)}) %reduce-scatter.3.cloned.1.call-update) | async-done | bytes 917520 | tf_op jit(solution)/shard_map/reduce_scatter | solution.py:91
  (54 shorter events, 6.4 us)
Async XLA Ops:
  7.2 1.5 copy-start.5
  7.2 4.3 %copy-start.2 = (bf16[384,896]{1,0:T(8,128)(2,1)S(1)}, bf16[384,896]{1,0:T(8,128)(2,1)}, u32[]{:S(2)}) copy-start(bf16[384,896]{1,0:T(8,128)(2,1)} %param.6) | copy-start | bytes 2064388
  7.2 39.1 %all-gather.5.cloned.1.call-start = ((), (), s32[]{:S(2)}) async-start(), calls=%async_computation.8 | async-start | bytes 2752512 | tf_op jit(solution)/shard_map/all_gather | solution.py:40
  7.9 66.2 %all-gather.7.cloned.1.call-start = ((), (), s32[]{:S(2)}) async-start(), calls=%async_computation.9 | async-start | bytes 2752512 | tf_op jit(solution)/shard_map/all_gather | solution.py:41
  9.7 19.4 %copy-start.6 = (s32[384,8]{0,1:T(8,128)S(1)}, s32[384,8]{0,1:T(8,128)}, u32[]{:S(2)}) copy-start(s32[384,8]{0,1:T(8,128)} %param.8) | copy-start | bytes 36868
  11.5 29.8 %copy-start.3 = (bf16[384,896]{1,0:T(8,128)(2,1)S(1)}, bf16[384,896]{1,0:T(8,128)(2,1)}, u32[]{:S(2)}) copy-start(bf16[384,896]{1,0:T(8,128)(2,1)} %param.11) | copy-start | bytes 2064388
  24.9 18.0 %all-to-all-start = ((bf16[4,24,896]{2,1,0:T(8,128)(2,1)}), bf16[4,24,896]{2,1,0:T(8,128)(2,1)S(1)}, u32[]{:S(2)}, u32[]{:S(2)}) async-start(bf16[4,24,896]{2,1,0:T(8,128)(2,1)} %bitcast.3), calls=%async_computation | async-start | bytes 344064 | tf_op jit(solution)/shard_map/all_to_all | solution.py:36
  42.9 8.4 %all-to-all-start.2 = ((bf16[4,24,896]{2,1,0:T(8,128)(2,1)}), bf16[4,24,896]{2,1,0:T(8,128)(2,1)S(1)}, u32[]{:S(2)}, u32[]{:S(2)}) async-start(bf16[4,24,896]{2,1,0:T(8,128)(2,1)} %fusion.19), calls=%async_computation.2 | async-start | bytes 344064 | tf_op jit(solution)/shard_map/all_to_all | solution.py:61
  46.3 74.9 %all-reduce.5.cloned.1.call-start = ((), (), s32[]{:S(2)}) async-start(), calls=%async_computation.10 | async-start | bytes 1572864 | tf_op jit(solution)/shard_map/psum | solution.py:43
  77.1 75.4 %reduce-scatter.5.cloned.1.call-start = ((), (), s32[]{:S(2)}) async-start(), calls=%async_computation.7 | async-start | bytes 2752512 | tf_op jit(solution)/shard_map/reduce_scatter | solution.py:94
  121.2 3.1 %copy-start.1 = (f32[96,1024]{1,0:T(8,128)S(1)}, f32[96,1024]{1,0:T(8,128)}, u32[]{:S(2)}) copy-start(f32[96,1024]{1,0:T(8,128)} %get-tuple-element.4) | copy-start | bytes 1179652
  121.2 3.1 %copy-start.4 = (f32[96,1024]{1,0:T(8,128)S(1)}, f32[96,1024]{1,0:T(8,128)}, u32[]{:S(2)}) copy-start(f32[96,1024]{1,0:T(8,128)} %get-tuple-element.5) | copy-start | bytes 1179652
  124.2 60.1 %reduce-scatter.3.cloned.1.call-start = ((), (), s32[]{:S(2)}) async-start(), calls=%async_computation.6 | async-start | bytes 2752512 | tf_op jit(solution)/shard_map/reduce_scatter | solution.py:91
  126.4 6.1 %copy-start = (bf16[1,896,1024]{2,1,0:T(8,128)(2,1)S(1)}, bf16[1,896,1024]{2,1,0:T(8,128)(2,1)}, u32[]{:S(2)}) copy-start(bf16[1,896,1024]{2,1,0:T(8,128)(2,1)} %all-gather.5.cloned.1.call-done) | copy-start | bytes 5505028
  129.1 8.4 %all-to-all-start.1 = ((bf16[4,24,896]{2,1,0:T(8,128)(2,1)}), bf16[4,24,896]{2,1,0:T(8,128)(2,1)S(1)}, u32[]{:S(2)}, u32[]{:S(2)}) async-start(bf16[4,24,896]{2,1,0:T(8,128)(2,1)} %bitcast.7), calls=%async_computation.1 | async-start | bytes 344064 | tf_op jit(solution)/shard_map/all_to_all | solution.py:46
  137.5 8.4 %all-to-all-start.3 = ((bf16[4,24,896]{2,1,0:T(8,128)(2,1)}), bf16[4,24,896]{2,1,0:T(8,128)(2,1)S(1)}, u32[]{:S(2)}, u32[]{:S(2)}) async-start(bf16[4,24,896]{2,1,0:T(8,128)(2,1)} %bitcast.11), calls=%async_computation.3 | async-start | bytes 344064 | tf_op jit(solution)/shard_map/all_to_all | solution.py:77
Sparse Core Ops, SparseCore 0:
  9.5 32.8 all-gather.4
  44.0 30.1 all-gather.6
  77.2 43.8 all-reduce.4
  124.3 28.2 reduce-scatter.4
  155.2 29.0 reduce-scatter.2
where the time goes:
time: 191 us
  waiting for transfers between devices  112 us (59%)
  local copies, waits for them, and re-layouts  29.3 us (15%)
  matrix products  14.6 us (8%)
  starting transfers between devices  14.5 us (8%)
  between operations  14.1 us (7%)
  other arithmetic  5.97 us (3%)
    psum x1, waiting for transfers between devices, body(): lax.psum(jnp.dot(arrived, w_up, preferred_element_type=jnp.float32), 'tp')  44 us
    reduce_scatter x1, waiting for transfers between devices, body(): lax.psum_scatter(part_up.astype(jnp.bfloat16), 'dp', scatter_dimension=1,...  31.7 us
    all_gather x1, waiting for transfers between devices, body(): lax.all_gather(down_weight[0], 'dp', axis=0, tiled=True)  22.8 us
    scatter x1, local copies, waits for them, and re-layouts, place_slots(): jnp.full((experts * capacity,), rows_count, jnp.int32).at[target]  11.8 us
    scatter x1, local copies, waits for them, and re-layouts, place_slots(): jnp.zeros((experts * capacity,), jnp.float32).at[target]  11.8 us
    all_to_all x1, starting transfers between devices, body(): lax.all_to_all(outgoing, 'ctx', split_axis=0, concat_axis=0, tiled=True)  4.26 us
    reduce_scatter x1, waiting for transfers between devices, body(): lax.psum_scatter(part_down.astype(jnp.bfloat16), 'dp', scatter_dimension=...  4.05 us
  transfers between devices with their start and end apart: 9, of which 7 were waited for; matrix products, arithmetic and copies ran while one was open for 23% of the time, Pallas kernels for 0%

commit v1 on v0

--- a/solution.py
+++ b/solution.py
@@ -2,6 +2,18 @@
 import jax.numpy as jnp
 from jax import lax
 from jax.sharding import PartitionSpec as P
+
+
+def gather_by_bits(shard, axis, dim):
+    ways, here = (lax.axis_size(axis), lax.axis_index(axis))
+    grown, reach = (shard, 1)
+    while reach < ways:
+        theirs = lax.ppermute(grown, axis, [(d, d ^ reach) for d in range(ways)])
+        mine_first = jnp.concatenate([grown, theirs], axis=dim)
+        theirs_first = jnp.concatenate([theirs, grown], axis=dim)
+        grown = jnp.where(here & reach == 0, mine_first, theirs_first)
+        reach = 2 * reach
+    return grown
 
 
 def place_slots(expert_ids, gate_codes, experts, capacity):
@@ -38,7 +50,7 @@
     )
     w_up, w_down = (
         lax.all_gather(up_weight[0], "dp", axis=1, tiled=True),
-        lax.all_gather(down_weight[0], "dp", axis=0, tiled=True),
+        gather_by_bits(down_weight[0], "dp", 0),
     )
     hidden = lax.psum(jnp.dot(arrived, w_up, preferred_element_type=jnp.float32), "tp")
     active = jax.nn.silu(hidden).astype(jnp.bfloat16)

time: 191 us -> 175 us (0.916)
  waiting for transfers between devices: 112 us -> 91 us
  starting transfers between devices: 14.5 us -> 16.7 us
    all_gather x1 -> x0, waiting for transfers between devices: 22.8 us -> none  [body(): lax.all_gather(down_weight[0], 'dp', axis=0, tiled=True)]
    ppermute x0 -> x1, starting transfers between devices: none -> 3.03 us  [gather_by_bits(): theirs = lax.ppermute(grown, axis, [(d, d ^ reach) for d in range(ways)])]
    all_to_all x1, waiting for transfers between devices: 0.01 us -> 1.93 us  [body(): lax.all_to_all(outgoing, 'ctx', split_axis=0, concat_axis=0, tiled=True)]
  transfers between devices with their start and end apart: 9 -> 9, of which waited for: 7 -> 7; matrix products, arithmetic and copies ran while one was open for 23% -> 27% of each run, Pallas kernels for 0% -> 0%
where the time goes in v1:
time: 175 us; the launch traced here: 174 us
  waiting for transfers between devices  91 us (52%)
  local copies, waits for them, and re-layouts  30 us (17%)
  starting transfers between devices  16.7 us (10%)
  matrix products  14.9 us (9%)
  between operations  14 us (8%)
  other arithmetic  7.38 us (4%)
    psum x1, waiting for transfers between devices, body(): lax.psum(jnp.dot(arrived, w_up, preferred_element_type=jnp.float32), 'tp')  43.3 us
    reduce_scatter x1, waiting for transfers between devices, body(): lax.psum_scatter(part_up.astype(jnp.bfloat16), 'dp', scatter_dimension=1,...  31.7 us
    scatter x1, local copies, waits for them, and re-layouts, place_slots(): jnp.zeros((experts * capacity,), jnp.float32).at[target]  11.8 us
    scatter x1, local copies, waits for them, and re-layouts, place_slots(): jnp.full((experts * capacity,), rows_count, jnp.int32).at[target]  11.8 us
    reduce_scatter x1, waiting for transfers between devices, body(): lax.psum_scatter(part_down.astype(jnp.bfloat16), 'dp', scatter_dimension=...  3.88 us
    all_to_all x1, waiting for transfers between devices, body(): lax.all_to_all(produced.reshape(sources, capacity, features), 'ctx', spli...  3.65 us
  transfers between devices with their start and end apart: 9, of which 7 were waited for; matrix products, arithmetic and copies ran while one was open for 27% of the time, Pallas kernels for 0%

profile of v1, /device:TPU:0, one launch (start us, length us, event | category | flops | bytes accessed | tf_op | source)
XLA Modules:
  0.0 174.1 jit_solution(3136138067605252014)
XLA Ops:
  7.9 3.0 %collective-permute-start = (bf16[512,896]{1,0:T(8,128)(2,1)}, bf16[512,896]{1,0:T(8,128)(2,1)}, u32[]{:S(2)}, u32[]{:S(2)}) collective-permute-start(bf16[512,896]{1,0:T(8,128)(2,1)} %bitcast.61), channel_id=1, source_target_pairs={{0,1},{1,0},{2,3},{3,2},{4,5},{5,4},{6,7},{7,6},{8,9},{9,8},{10,11... | collective-permute-start | bytes 2752520 | tf_op jit(solution)/shard_map/ppermute | solution.py:11
  14.1 1.2 reduce-window.6
  16.2 11.8 %scatter_custom_fusion.1 = f32[96]{0:T(128)S(1)} fusion(s32[3072]{0:T(1024)S(1)} %bitcast.58, f32[3072]{0:T(1024)S(1)} %reshape.139, f32[]{:T(128)} %constant.16.clone.1), kind=kCustom, calls=%fused_computation.52 | custom fusion | bytes 388 | tf_op jit(solution)/shard_map/scatter | solution.py:32
  28.0 11.8 %scatter_custom_fusion = s32[96]{0:T(128)S(1)} fusion(s32[3072]{0:T(1024)S(1)} %bitcast.59, s32[3072]{0:T(1024)S(1)} %add_select_fusion, s32[]{:T(128)} %constant.17.clone.1), kind=kCustom, calls=%fused_computation.54 | custom fusion | bytes 388 | tf_op jit(solution)/shard_map/scatter | solution.py:29
  41.5 3.5 %all-to-all-start.2 = ((bf16[4,24,896]{2,1,0:T(8,128)(2,1)}), bf16[4,24,896]{2,1,0:T(8,128)(2,1)S(1)}, u32[]{:S(2)}, u32[]{:S(2)}) async-start(bf16[4,24,896]{2,1,0:T(8,128)(2,1)} %fusion.12), calls=%async_computation.2 | async-start | bytes 344064 | tf_op jit(solution)/shard_map/all_to_all | solution.py:73
  45.0 1.5 gather_fusion
  46.5 3.5 %all-to-all-done.2 = bf16[4,24,896]{2,1,0:T(8,128)(2,1)S(1)} async-done(((bf16[4,24,896]{2,1,0:T(8,128)(2,1)}), bf16[4,24,896]{2,1,0:T(8,128)(2,1)S(1)}, u32[]{:S(2)}, u32[]{:S(2)}) %all-to-all-start.2) | async-done | bytes 172064 | tf_op jit(solution)/shard_map/all_to_all | solution.py:73
  50.0 3.4 %all-to-all-start = ((bf16[4,24,896]{2,1,0:T(8,128)(2,1)}), bf16[4,24,896]{2,1,0:T(8,128)(2,1)S(1)}, u32[]{:S(2)}, u32[]{:S(2)}) async-start(bf16[4,24,896]{2,1,0:T(8,128)(2,1)} %bitcast.3), calls=%async_computation | async-start | bytes 344064 | tf_op jit(solution)/shard_map/all_to_all | solution.py:48
  53.4 3.0 %fusion.13 = f32[96,1024]{1,0:T(8,128)} fusion(bf16[96,896]{1,0:T(8,128)(2,1)S(1)} %bitcast.52, bf16[512,896]{1,0:T(8,128)(2,1)} %collective-permute-done, bf16[512,896]{1,0:T(8,128)(2,1)S(1)} %bitcast.62, pred[]{:T(512)S(6)} %eq.36), kind=kOutput, calls=%fused_computation.28 | convolution fusion | flops 184418304 | bytes 2400257 | tf_op jit(solution)/shard_map/dot_general | solution.py:83
  56.4 1.9 %all-to-all-done = bf16[4,24,896]{2,1,0:T(8,128)(2,1)S(1)} async-done(((bf16[4,24,896]{2,1,0:T(8,128)(2,1)}), bf16[4,24,896]{2,1,0:T(8,128)(2,1)S(1)}, u32[]{:S(2)}, u32[]{:S(2)}) %all-to-all-start) | async-done | bytes 172064 | tf_op jit(solution)/shard_map/all_to_all | solution.py:48
  58.3 2.7 %fusion.2 = f32[96,1024]{1,0:T(8,128)} fusion(bf16[96,896]{1,0:T(8,128)(2,1)S(1)} %bitcast.50, bf16[1,896,1024]{2,1,0:T(8,128)(2,1)} %all-gather.3.cloned.1.call-done), kind=kOutput, calls=%fused_computation.9 | convolution fusion | flops 176160768 | bytes 2400256 | tf_op jit(solution)/shard_map/dot_general | solution.py:55
  61.1 43.3 %all-reduce.5.cloned.1.call-done = (f32[96,1024]{1,0:T(8,128)}, f32[96,1024]{1,0:T(8,128)}) async-done(((f32[96,1024]{1,0:T(8,128)}, f32[96,1024]{1,0:T(8,128)}), (f32[96,1024]{1,0:T(8,128)}, f32[96,1024]{1,0:T(8,128)})) %all-reduce.5.cloned.1.call-update) | async-done | bytes 786448 | tf_op jit(solution)/shard_map/psum | solution.py:55
  104.4 3.0 %convolution_convert_fusion = bf16[1024,896]{1,0:T(8,128)(2,1)} fusion(bf16[96,896]{1,0:T(8,128)(2,1)S(1)} %bitcast.53, f32[96,1024]{1,0:T(8,128)} %get-tuple-element.4), kind=kOutput, calls=%fused_computation.11 | convolution fusion | flops 177569792 | bytes 2400256 | tf_op jit(solution)/shard_map/dot_general | solution.py:99
  107.7 1.9 %convolution_convert_fusion.1 = bf16[896,1024]{1,0:T(8,128)(2,1)} fusion(bf16[96,896]{1,0:T(8,128)(2,1)S(1)} %bitcast.51, bf16[96,1024]{1,0:T(8,128)(2,1)S(1)} %multiply_convert_fusion), kind=kOutput, calls=%fused_computation.12 | convolution fusion | flops 177078272 | bytes 2203648 | tf_op jit(solution)/shard_map/dot_general | solution.py:98
  109.6 3.0 %convolution_convert_fusion.2 = bf16[96,896]{1,0:T(8,128)(2,1)} fusion(bf16[512,896]{1,0:T(8,128)(2,1)} %collective-permute-done, bf16[512,896]{1,0:T(8,128)(2,1)S(1)} %bitcast.63, pred[]{:T(512)S(6)} %eq.36, f32[96,1024]{1,0:T(8,128)S(1)} %copy-done.1), kind=kOutput, calls=%fused_computation.16 | convolution fusion | flops 184995840 | bytes 2400257 | tf_op jit(solution)/shard_map/dot_general | solution.py:57
  112.6 3.4 %all-to-all-start.1 = ((bf16[4,24,896]{2,1,0:T(8,128)(2,1)}), bf16[4,24,896]{2,1,0:T(8,128)(2,1)S(1)}, u32[]{:S(2)}, u32[]{:S(2)}) async-start(bf16[4,24,896]{2,1,0:T(8,128)(2,1)} %bitcast.7), calls=%async_computation.1 | async-start | bytes 344064 | tf_op jit(solution)/shard_map/all_to_all | solution.py:58
  116.0 1.3 fusion.4
  117.3 3.6 %all-to-all-done.1 = bf16[4,24,896]{2,1,0:T(8,128)(2,1)S(1)} async-done(((bf16[4,24,896]{2,1,0:T(8,128)(2,1)}), bf16[4,24,896]{2,1,0:T(8,128)(2,1)S(1)}, u32[]{:S(2)}, u32[]{:S(2)}) %all-to-all-start.1) | async-done | bytes 172064 | tf_op jit(solution)/shard_map/all_to_all | solution.py:58
  121.0 3.3 %all-to-all-start.3 = ((bf16[4,24,896]{2,1,0:T(8,128)(2,1)}), bf16[4,24,896]{2,1,0:T(8,128)(2,1)S(1)}, u32[]{:S(2)}, u32[]{:S(2)}) async-start(bf16[4,24,896]{2,1,0:T(8,128)(2,1)} %bitcast.11), calls=%async_computation.3 | async-start | bytes 344064 | tf_op jit(solution)/shard_map/all_to_all | solution.py:89
  124.3 1.8 %scatter_custom_fusion.2 = f32[385,896]{1,0:T(8,128)S(1)} fusion(s32[96]{0:T(128)S(1)} %compare_select_fusion.1, f32[]{:T(128)} %constant.16.clone.1, bf16[96,896]{1,0:T(8,128)(2,1)S(1)} %bitcast.54, f32[96]{0:T(128)S(1)} %scatter_custom_fusion.1), kind=kCustom, calls=%fused_computation.19 | custom fusion | flops 258048 | bytes 1552388 | tf_op jit(solution)/shard_map/scatter-add | solution.py:68
  127.0 2.3 %all-to-all-done.3 = bf16[4,24,896]{2,1,0:T(8,128)(2,1)S(1)} async-done(((bf16[4,24,896]{2,1,0:T(8,128)(2,1)}), bf16[4,24,896]{2,1,0:T(8,128)(2,1)S(1)}, u32[]{:S(2)}, u32[]{:S(2)}) %all-to-all-start.3) | async-done | bytes 172064 | tf_op jit(solution)/shard_map/all_to_all | solution.py:89
  129.3 1.7 scatter_custom_fusion.3
  132.0 3.9 %reduce-scatter.5.cloned.1.call-done = bf16[512,896]{1,0:T(8,128)(2,1)} async-done(((bf16[1024,896]{1,0:T(8,128)(2,1)}), bf16[512,896]{1,0:T(8,128)(2,1)}) %reduce-scatter.5.cloned.1.call-update) | async-done | bytes 917520 | tf_op jit(solution)/shard_map/reduce_scatter | solution.py:106
  135.8 31.7 %reduce-scatter.3.cloned.1.call-done = bf16[896,512]{1,0:T(8,128)(2,1)} async-done(((bf16[896,1024]{1,0:T(8,128)(2,1)}), bf16[896,512]{1,0:T(8,128)(2,1)}) %reduce-scatter.3.cloned.1.call-update) | async-done | bytes 917520 | tf_op jit(solution)/shard_map/reduce_scatter | solution.py:103
  (53 shorter events, 8.7 us)
Async XLA Ops:
  7.2 8.7 %copy-start.5 = (s32[384,8]{0,1:T(8,128)S(1)}, s32[384,8]{0,1:T(8,128)}, u32[]{:S(2)}) copy-start(s32[384,8]{0,1:T(8,128)} %param.8) | copy-start | bytes 36868
  7.2 32.6 %copy-start.2 = (bf16[384,896]{1,0:T(8,128)(2,1)S(1)}, bf16[384,896]{1,0:T(8,128)(2,1)}, u32[]{:S(2)}) copy-start(bf16[384,896]{1,0:T(8,128)(2,1)} %param.11) | copy-start | bytes 2064388
  7.2 51.1 %all-gather.3.cloned.1.call-start = ((), (), s32[]{:S(2)}) async-start(), calls=%async_computation.8 | async-start | bytes 2752512 | tf_op jit(solution)/shard_map/all_gather | solution.py:52
  7.9 45.5 %collective-permute-start = (bf16[512,896]{1,0:T(8,128)(2,1)}, bf16[512,896]{1,0:T(8,128)(2,1)}, u32[]{:S(2)}, u32[]{:S(2)}) collective-permute-start(bf16[512,896]{1,0:T(8,128)(2,1)} %bitcast.61), channel_id=1, source_target_pairs={{0,1},{1,0},{2,3},{3,2},{4,5},{5,4},{6,7},{7,6},{8,9},{9,8},{10,11... | collective-permute-start | bytes 2752520 | tf_op jit(solution)/shard_map/ppermute | solution.py:11
  16.1 28.8 %copy-start.3 = (bf16[384,896]{1,0:T(8,128)(2,1)S(1)}, bf16[384,896]{1,0:T(8,128)(2,1)}, u32[]{:S(2)}) copy-start(bf16[384,896]{1,0:T(8,128)(2,1)} %param.6) | copy-start | bytes 2064388
  41.5 11.9 %copy-start.6 = (bf16[1,512,896]{2,1,0:T(8,128)(2,1)S(1)}, bf16[1,512,896]{2,1,0:T(8,128)(2,1)}, u32[]{:S(2)}) copy-start(bf16[1,512,896]{2,1,0:T(8,128)(2,1)} %param.10) | copy-start | bytes 2752516
  41.5 8.5 %all-to-all-start.2 = ((bf16[4,24,896]{2,1,0:T(8,128)(2,1)}), bf16[4,24,896]{2,1,0:T(8,128)(2,1)S(1)}, u32[]{:S(2)}, u32[]{:S(2)}) async-start(bf16[4,24,896]{2,1,0:T(8,128)(2,1)} %fusion.12), calls=%async_computation.2 | async-start | bytes 344064 | tf_op jit(solution)/shard_map/all_to_all | solution.py:73
  50.0 8.4 %all-to-all-start = ((bf16[4,24,896]{2,1,0:T(8,128)(2,1)}), bf16[4,24,896]{2,1,0:T(8,128)(2,1)S(1)}, u32[]{:S(2)}, u32[]{:S(2)}) async-start(bf16[4,24,896]{2,1,0:T(8,128)(2,1)} %bitcast.3), calls=%async_computation | async-start | bytes 344064 | tf_op jit(solution)/shard_map/all_to_all | solution.py:48
  53.3 51.1 %all-reduce.5.cloned.1.call-start = ((), (), s32[]{:S(2)}) async-start(), calls=%async_computation.9 | async-start | bytes 1572864 | tf_op jit(solution)/shard_map/psum | solution.py:55
  61.1 74.8 %reduce-scatter.5.cloned.1.call-start = ((), (), s32[]{:S(2)}) async-start(), calls=%async_computation.7 | async-start | bytes 2752512 | tf_op jit(solution)/shard_map/reduce_scatter | solution.py:106
  104.4 3.1 %copy-start.1 = (f32[96,1024]{1,0:T(8,128)S(1)}, f32[96,1024]{1,0:T(8,128)}, u32[]{:S(2)}) copy-start(f32[96,1024]{1,0:T(8,128)} %get-tuple-element.4) | copy-start | bytes 1179652
  104.4 3.1 %copy-start.4 = (f32[96,1024]{1,0:T(8,128)S(1)}, f32[96,1024]{1,0:T(8,128)}, u32[]{:S(2)}) copy-start(f32[96,1024]{1,0:T(8,128)} %get-tuple-element.5) | copy-start | bytes 1179652
  107.5 60.1 %reduce-scatter.3.cloned.1.call-start = ((), (), s32[]{:S(2)}) async-start(), calls=%async_computation.6 | async-start | bytes 2752512 | tf_op jit(solution)/shard_map/reduce_scatter | solution.py:103
  109.6 6.3 %copy-start = (bf16[1,896,1024]{2,1,0:T(8,128)(2,1)S(1)}, bf16[1,896,1024]{2,1,0:T(8,128)(2,1)}, u32[]{:S(2)}) copy-start(bf16[1,896,1024]{2,1,0:T(8,128)(2,1)} %all-gather.3.cloned.1.call-done) | copy-start | bytes 5505028
  112.6 8.4 %all-to-all-start.1 = ((bf16[4,24,896]{2,1,0:T(8,128)(2,1)}), bf16[4,24,896]{2,1,0:T(8,128)(2,1)S(1)}, u32[]{:S(2)}, u32[]{:S(2)}) async-start(bf16[4,24,896]{2,1,0:T(8,128)(2,1)} %bitcast.7), calls=%async_computation.1 | async-start | bytes 344064 | tf_op jit(solution)/shard_map/all_to_all | solution.py:58
  121.0 8.4 %all-to-all-start.3 = ((bf16[4,24,896]{2,1,0:T(8,128)(2,1)}), bf16[4,24,896]{2,1,0:T(8,128)(2,1)S(1)}, u32[]{:S(2)}, u32[]{:S(2)}) async-start(bf16[4,24,896]{2,1,0:T(8,128)(2,1)} %bitcast.11), calls=%async_computation.3 | async-start | bytes 344064 | tf_op jit(solution)/shard_map/all_to_all | solution.py:89
Sparse Core Ops, SparseCore 0:
  9.5 41.8 all-gather.2
  61.2 43.2 all-reduce.4
  107.6 28.2 reduce-scatter.4
  138.5 29.0 reduce-scatter.2
